TPU v7x, 128 devices: a whole 4x4x4 slice. The times are simulated.
128 devices in a mesh: ex: 8 (over y, x_hi), pb: 16 (over z, x_lo, core).
Axes of the slice: x: 4 (x_hi: 2, x_lo: 2; x = x_hi * 2 + x_lo), y: 4, z: 4, core: 2. Of those that a mesh axis runs over, the one named last changes fastest.
Arguments:
- train_features: bfloat16 [131072, 4096], P('ex', 'pb'), may hold values from -6 to 6
- query_features: bfloat16 [2048, 4096], P('ex', 'pb'), may hold values from -6 to 6
- precond: bfloat16 [4096, 4096], P('pb'), may hold values from -0.09375 to 0.09375
- example_weight: float32 [131072], P(('ex', 'pb')), may hold values from 0.05 to 0.95
- select: int32 [16, 1024], P(None, ('ex', 'pb')), may hold values from 0 to 1, as said below
Outputs:
- scores: float32 [2048, 131072], P(None, ('ex', 'pb'))
Inputs may be any that keep to these rules, and one draw needn't show every extreme that they name: `select`: 1 where the pair of query block and training block is to be scored, else 0; the number of listed pairs differs widely between query blocks and between training blocks.
All inputs are finite; a program needn't handle non-finite values.
Results may differ from a plain program's by a relative error of at most 0.0029.
Values may be sent and summed in bfloat16 or wider, within the bound.
No kernel may reach another device: no remote copies, remote signals or barrier semaphores. Data moves between devices by JAX's collectives and lax.ppermute only.
A program may use at most 128 MiB of HBM per device.

v0:
```python
import jax
import jax.numpy as jnp
from jax import lax
from jax.sharding import PartitionSpec as P

BLK = 128


def tile_product(portion, train_tile):
    return lax.dot_general(
        portion, train_tile, (((1,), (1,)), ((), ())), preferred_element_type=jnp.float32
    )


def on_device(train_features, query_features, precond, example_weight, select):
    rows_here = lax.all_to_all(train_features, "pb", split_axis=0, concat_axis=1, tiled=True)
    feature_width = rows_here.shape[1]
    gathered = lax.psum(
        jnp.dot(query_features, precond, preferred_element_type=jnp.float32), "pb"
    ).astype(jnp.bfloat16)
    block_count = select.shape[0]
    train_blocks = select.shape[1]
    product_part = tile_product(lax.all_gather(gathered, "ex", axis=0, tiled=True), rows_here)
    scaled = product_part * feature_width ** (-0.5) * example_weight[None, :]
    keep_mask = select.astype(jnp.float32)
    masked = scaled.reshape(block_count, BLK, train_blocks, BLK) * keep_mask[:, None, :, None]
    return masked.reshape(product_part.shape)


def solution(mesh):
    placed = (P("ex", "pb"), P("ex", "pb"), P("pb", None), P(("ex", "pb")), P(None, ("ex", "pb")))
    return jax.shard_map(
        on_device, mesh=mesh, in_specs=placed, out_specs=P(None, ("ex", "pb")), check_vma=False
    )
```

profile of v0, /device:TPU:1, one launch (start us, length us, event | category | flops | bytes accessed | tf_op | source)
XLA Modules:
  0.0 383.1 jit_solution(517960048451074875)
XLA Ops:
  6.5 0.0 copy-start
  6.5 0.0 all-gather.2.cloned.1.call-start
  6.5 1.6 copy-done
  8.1 3.6 fusion
  11.8 97.5 %all-reduce.1 = bf16[256,4096]{1,0:T(8,128)(2,1)} all-reduce(f32[256,4096]{1,0:T(8,128)} %fusion), channel_id=1, replica_groups=mesh['ex'=8,'pb'=16] {'pb'}, use_global_device_ids=true, to_apply=%region_0.0 | all-reduce | flops 1048576 | bytes 6291456 | tf_op jit(solution)/shard_map/psum | solution.py:18
  109.3 0.0 all-gather.2.cloned.1.call-update
  109.3 0.0 copy-start.3
  109.3 0.0 copy-start.4
  109.3 7.5 %all-to-all-start = ((bf16[16,1024,256]{2,1,0:T(8,128)(2,1)}), bf16[16,1024,256]{2,1,0:T(8,128)(2,1)}, u32[]{:S(2)}, u32[]{:S(2)}) async-start(bf16[16,1024,256]{2,1,0:T(8,128)(2,1)} %bitcast.12), calls=%async_computation | async-start | bytes 16777216 | tf_op jit(solution)/shard_map/all_to_all | solution.py:16
  116.8 0.0 copy-done.3
  116.8 0.1 copy.9
  116.9 0.0 copy-done.4
  116.9 150.3 %all-to-all-done = bf16[16,1024,256]{2,1,0:T(8,128)(2,1)} async-done(((bf16[16,1024,256]{2,1,0:T(8,128)(2,1)}), bf16[16,1024,256]{2,1,0:T(8,128)(2,1)}, u32[]{:S(2)}, u32[]{:S(2)}) %all-to-all-start) | async-done | bytes 8388640 | tf_op jit(solution)/shard_map/all_to_all | solution.py:16
  267.2 12.2 %copy.8 = bf16[1024,16,256]{0,2,1:T(8,128)(2,1)} copy(bf16[1024,16,256]{2,0,1:T(8,128)(2,1)} %bitcast.1) | data formatting | bytes 16777216 | tf_op jit(solution)/shard_map/all_to_all | solution.py:16
  279.5 70.8 %all-gather.2.cloned.1.call-done = bf16[2048,4096]{1,0:T(8,128)(2,1)} async-done(((bf16[256,4096]{1,0:T(8,128)(2,1)}), bf16[2048,4096]{1,0:T(8,128)(2,1)}) %all-gather.2.cloned.1.call-update) | async-done | bytes 16777232 | tf_op jit(solution)/shard_map/all_gather | solution.py:23
  350.3 0.0 copy-start.2
  350.3 0.6 mul.29
  350.9 2.8 copy-done.2
  353.7 0.0 copy-start.1
  353.7 22.6 %bitcast_multiply_fusion = f32[2048,1024]{1,0:T(8,128)} fusion(f32[256,8,8,128]{3,2,1,0:T(8,128)S(1)} %bitcast.11, bf16[2048,4096]{1,0:T(8,128)(2,1)} %all-gather.2.cloned.1.call-done, bf16[1024,4096]{0,1:T(8,128)(2,1)S(1)} %bitcast.13, f32[1024]{0:T(1024)S(1)} %broadcast_multiply_fusion), kind=kOutput, calls=%fused_computation | convolution fusion | flops 17184063488 | bytes 41947136 | tf_op jit(solution)/shard_map/dot_general | solution.py:10
  376.3 0.0 copy-done.1
  (2 shorter events, 0.0 us)
Async XLA Ops:
  6.5 1.6 copy-start
  6.5 343.8 %all-gather.2.cloned.1.call-start = ((), (), s32[]{:S(2)}) async-start(), calls=%async_computation.1 | async-start | bytes 18874368 | tf_op jit(solution)/shard_map/all_gather | solution.py:23
  109.3 7.5 %copy-start.3 = (s32[16,8]{0,1:T(8,128)S(1)}, s32[16,8]{0,1:T(8,128)}, u32[]{:S(2)}) copy-start(s32[16,8]{0,1:T(8,128)} %param.9) | copy-start | bytes 1540
  109.3 7.6 %copy-start.4 = (f32[1024]{0:T(1024)S(1)}, f32[1024]{0:T(1024)}, u32[]{:S(2)}) copy-start(f32[1024]{0:T(1024)} %param.8) | copy-start | bytes 12292
  109.3 157.9 %all-to-all-start = ((bf16[16,1024,256]{2,1,0:T(8,128)(2,1)}), bf16[16,1024,256]{2,1,0:T(8,128)(2,1)}, u32[]{:S(2)}, u32[]{:S(2)}) async-start(bf16[16,1024,256]{2,1,0:T(8,128)(2,1)} %bitcast.12), calls=%async_computation | async-start | bytes 16777216 | tf_op jit(solution)/shard_map/all_to_all | solution.py:16
  350.3 3.4 copy-start.2
  353.7 22.6 %copy-start.1 = (bf16[256,4096]{1,0:T(8,128)(2,1)S(1)}, bf16[256,4096]{1,0:T(8,128)(2,1)}, u32[]{:S(2)}) copy-start(bf16[256,4096]{1,0:T(8,128)(2,1)} %param.7) | copy-start | bytes 6291460
Sparse Core Ops, SparseCore 0:
  109.4 240.8 all-gather.1
where the time goes:
time: 384 us; the launch traced here: 383 us
  waiting for transfers between devices  221 us (58%)
  blocking collectives  97.5 us (25%)
  matrix products  26.2 us (7%)
  local copies, waits for them, and re-layouts  17.3 us (5%)
  between operations  13.4 us (3%)
  starting transfers between devices  7.52 us (2%)
    all_to_all x1, waiting for transfers between devices, on_device(): lax.all_to_all(train_features, 'pb', split_axis=0, concat_axis=1, tiled=T...  150 us
    psum x1, blocking collectives, on_device(): lax.psum(jnp.dot(query_features, precond, preferred_element_type=jnp.floa...  97.5 us
    all_gather x1, waiting for transfers between devices, on_device(): lax.all_gather(gathered, 'ex', axis=0, tiled=True)  70.8 us
    dot_general x1, matrix products, tile_product(): lax.dot_general(portion, train_tile, (((1,), (1,)), ((), ())), preferred_...  22.6 us
    all_to_all x1, local copies, waits for them, and re-layouts, on_device(): lax.all_to_all(train_features, 'pb', split_axis=0, concat_axis=1, tiled=T...  12.2 us
  transfers between devices with their start and end apart: 2, of which 2 were waited for; matrix products, arithmetic and copies ran while one was open for 3% of the time, Pallas kernels for 0%

commit v1 on v0

--- a/solution.py
+++ b/solution.py
@@ -20,7 +20,12 @@
     ).astype(jnp.bfloat16)
     block_count = select.shape[0]
     train_blocks = select.shape[1]
-    product_part = tile_product(lax.all_gather(gathered, "ex", axis=0, tiled=True), rows_here)
+    product_part = tile_product(
+        jnp.concatenate(
+            lax.all_to_all(jnp.stack([gathered] * lax.axis_size("ex")), "ex", 0, 0), axis=0
+        ),
+        rows_here,
+    )
     scaled = product_part * feature_width ** (-0.5) * example_weight[None, :]
     keep_mask = select.astype(jnp.float32)
     masked = scaled.reshape(block_count, BLK, train_blocks, BLK) * keep_mask[:, None, :, None]

time: 384 us -> 412 us (1.073)
  blocking collectives: 97.5 us -> 177 us
  waiting for transfers between devices: 221 us -> 171 us
  between operations: 13.4 us -> 0.06 us
  starting transfers between devices: 7.52 us -> 14.4 us
  local copies, waits for them, and re-layouts: 17.3 us -> 21.7 us
    all_to_all x0 -> x1, waiting for transfers between devices: none -> 171 us  [on_device(): lax.all_to_all(jnp.stack([gathered] * lax.axis_size('ex')), 'ex', 0, 0)]
    all_to_all x1, waiting for transfers between devices: 150 us -> 0.01 us  [on_device(): lax.all_to_all(train_features, 'pb', split_axis=0, concat_axis=1, tiled=T...]
    psum x1, blocking collectives: 97.5 us -> 177 us  [on_device(): lax.psum(jnp.dot(query_features, precond, preferred_element_type=jnp.floa...]
    all_gather x1 -> x0, waiting for transfers between devices: 70.8 us -> none  [on_device(): lax.all_gather(gathered, 'ex', axis=0, tiled=True)]
    all_to_all x0 -> x1, starting transfers between devices: none -> 6.49 us  [on_device(): lax.all_to_all(jnp.stack([gathered] * lax.axis_size('ex')), 'ex', 0, 0)]
    another operation x0 -> x1, local copies, waits for them, and re-layouts: none -> 5.97 us  [on_device(): jnp.stack([gathered] * lax.axis_size('ex'))]
  transfers between devices with their start and end apart: 2 -> 2, of which waited for: 2 -> 1; matrix products, arithmetic and copies ran while one was open for 3% -> 4% of each run, Pallas kernels for 0% -> 0%
where the time goes in v1:
time: 412 us; the launch traced here: 409 us
  blocking collectives  177 us (43%)
  waiting for transfers between devices  171 us (42%)
  matrix products  25.3 us (6%)
  local copies, waits for them, and re-layouts  21.7 us (5%)
  starting transfers between devices  14.4 us (3%)
    psum x1, blocking collectives, on_device(): lax.psum(jnp.dot(query_features, precond, preferred_element_type=jnp.floa...  177 us
    all_to_all x1, waiting for transfers between devices, on_device(): lax.all_to_all(jnp.stack([gathered] * lax.axis_size('ex')), 'ex', 0, 0)  171 us
    dot_general x1, matrix products, tile_product(): lax.dot_general(portion, train_tile, (((1,), (1,)), ((), ())), preferred_...  22.6 us
    all_to_all x1, local copies, waits for them, and re-layouts, on_device(): lax.all_to_all(train_features, 'pb', split_axis=0, concat_axis=1, tiled=T...  12.2 us
  transfers between devices with their start and end apart: 2, of which 1 were waited for; matrix products, arithmetic and copies ran while one was open for 4% of the time, Pallas kernels for 0%

profile of v1, /device:TPU:1, one launch (start us, length us, event | category | flops | bytes accessed | tf_op | source)
XLA Modules:
  0.0 409.2 jit_solution(17173161269915468544)
XLA Ops:
  0.0 0.0 copy-start
  0.0 0.0 copy-start.3
  0.0 7.9 %all-to-all-start.1 = ((bf16[16,1024,256]{2,1,0:T(8,128)(2,1)}), bf16[16,1024,256]{2,1,0:T(8,128)(2,1)}, u32[]{:S(2)}, u32[]{:S(2)}) async-start(bf16[16,1024,256]{2,1,0:T(8,128)(2,1)} %bitcast.13), calls=%async_computation.1 | async-start | bytes 16777216 | tf_op jit(solution)/shard_map/all_to_all | solution.py:16
  7.9 0.0 copy-done
  7.9 0.0 copy-done.3
  7.9 2.7 fusion
  10.6 177.2 %all-reduce.1 = bf16[256,4096]{1,0:T(8,128)(2,1)S(1)} all-reduce(f32[256,4096]{1,0:T(8,128)} %fusion), channel_id=1, replica_groups=mesh['ex'=8,'pb'=16] {'pb'}, use_global_device_ids=true, to_apply=%region_0.0 | all-reduce | flops 1048576 | bytes 6291456 | tf_op jit(solution)/shard_map/psum | solution.py:18
  187.9 0.0 all-to-all-done.1
  187.9 6.0 %stack.2 = bf16[8,256,4096]{2,1,0:T(8,128)(2,1)} broadcast(bf16[256,4096]{1,0:T(8,128)(2,1)S(1)} %all-reduce.1), dimensions={1,2} | broadcast | bytes 18874368 | tf_op jit(solution)/shard_map/stack | solution.py:25
  193.9 0.0 copy-start.4
  193.9 0.0 copy-start.5
  193.9 6.5 %all-to-all-start = ((bf16[8,256,4096]{2,1,0:T(8,128)(2,1)}), bf16[8,256,4096]{2,1,0:T(8,128)(2,1)}, u32[]{:S(2)}, u32[]{:S(2)}) async-start(bf16[8,256,4096]{2,1,0:T(8,128)(2,1)} %stack.2), calls=%async_computation | async-start | bytes 33554432 | tf_op jit(solution)/shard_map/all_to_all | solution.py:25
  200.4 0.0 copy-done.4
  200.4 0.1 copy.9
  200.4 0.0 copy-done.5
  200.4 12.2 %copy.8 = bf16[1024,16,256]{0,2,1:T(8,128)(2,1)} copy(bf16[1024,16,256]{2,0,1:T(8,128)(2,1)} %bitcast.2) | data formatting | bytes 16777216 | tf_op jit(solution)/shard_map/all_to_all | solution.py:16
  212.7 170.5 %all-to-all-done = bf16[8,256,4096]{2,1,0:T(8,128)(2,1)} async-done(((bf16[8,256,4096]{2,1,0:T(8,128)(2,1)}), bf16[8,256,4096]{2,1,0:T(8,128)(2,1)}, u32[]{:S(2)}, u32[]{:S(2)}) %all-to-all-start) | async-done | bytes 16777248 | tf_op jit(solution)/shard_map/all_to_all | solution.py:25
  383.2 0.0 copy-start.2
  383.2 0.6 mul.29
  383.8 2.8 copy-done.2
  386.6 0.0 copy-start.1
  386.6 22.6 %bitcast_multiply_fusion = f32[2048,1024]{1,0:T(8,128)} fusion(f32[256,8,8,128]{3,2,1,0:T(8,128)S(1)} %bitcast.12, bf16[2048,4096]{1,0:T(8,128)(2,1)} %bitcast, bf16[1024,4096]{0,1:T(8,128)(2,1)S(1)} %bitcast.14, f32[1024]{0:T(1024)S(1)} %broadcast_multiply_fusion), kind=kOutput, calls=%fused_computation | convolution fusion | flops 17184063488 | bytes 41947136 | tf_op jit(solution)/shard_map/dot_general | solution.py:10
  409.2 0.0 copy-done.1
  (2 shorter events, 0.0 us)
Async XLA Ops:
  0.0 7.9 %copy-start = (bf16[256,4096]{1,0:T(8,128)(2,1)S(1)}, bf16[256,4096]{1,0:T(8,128)(2,1)}, u32[]{:S(2)}) copy-start(bf16[256,4096]{1,0:T(8,128)(2,1)} %param.7) | copy-start | bytes 6291460
  0.0 7.9 %copy-start.3 = (bf16[256,256]{1,0:T(8,128)(2,1)S(1)}, bf16[256,256]{1,0:T(8,128)(2,1)}, u32[]{:S(2)}) copy-start(bf16[256,256]{1,0:T(8,128)(2,1)} %param.6) | copy-start | bytes 393220
  0.0 187.9 %all-to-all-start.1 = ((bf16[16,1024,256]{2,1,0:T(8,128)(2,1)}), bf16[16,1024,256]{2,1,0:T(8,128)(2,1)}, u32[]{:S(2)}, u32[]{:S(2)}) async-start(bf16[16,1024,256]{2,1,0:T(8,128)(2,1)} %bitcast.13), calls=%async_computation.1 | async-start | bytes 16777216 | tf_op jit(solution)/shard_map/all_to_all | solution.py:16
  193.9 6.5 %copy-start.4 = (s32[16,8]{0,1:T(8,128)S(1)}, s32[16,8]{0,1:T(8,128)}, u32[]{:S(2)}) copy-start(s32[16,8]{0,1:T(8,128)} %param.9) | copy-start | bytes 1540
  193.9 6.6 %copy-start.5 = (f32[1024]{0:T(1024)S(1)}, f32[1024]{0:T(1024)}, u32[]{:S(2)}) copy-start(f32[1024]{0:T(1024)} %param.8) | copy-start | bytes 12292
  193.9 189.4 %all-to-all-start = ((bf16[8,256,4096]{2,1,0:T(8,128)(2,1)}), bf16[8,256,4096]{2,1,0:T(8,128)(2,1)}, u32[]{:S(2)}, u32[]{:S(2)}) async-start(bf16[8,256,4096]{2,1,0:T(8,128)(2,1)} %stack.2), calls=%async_computation | async-start | bytes 33554432 | tf_op jit(solution)/shard_map/all_to_all | solution.py:25
  383.2 3.4 copy-start.2
  386.6 22.6 %copy-start.1 = (bf16[256,4096]{1,0:T(8,128)(2,1)S(1)}, bf16[256,4096]{1,0:T(8,128)(2,1)}, u32[]{:S(2)}) copy-start(bf16[256,4096]{1,0:T(8,128)(2,1)} %param.7) | copy-start | bytes 6291460

commit v2 on v0

--- a/solution.py
+++ b/solution.py
@@ -15,8 +15,9 @@
 def on_device(train_features, query_features, precond, example_weight, select):
     rows_here = lax.all_to_all(train_features, "pb", split_axis=0, concat_axis=1, tiled=True)
     feature_width = rows_here.shape[1]
-    gathered = lax.psum(
-        jnp.dot(query_features, precond, preferred_element_type=jnp.float32), "pb"
+    gathered = jnp.sum(
+        lax.all_gather(jnp.dot(query_features, precond, preferred_element_type=jnp.float32), "pb"),
+        axis=0,
     ).astype(jnp.bfloat16)
     block_count = select.shape[0]
     train_blocks = select.shape[1]

time: 384 us -> 638 us (1.66)
  waiting for transfers between devices: 221 us -> 554 us
  blocking collectives: 97.5 us -> 0 us
  other arithmetic: 0.01 us -> 22.4 us
    all_gather x0 -> x1, waiting for transfers between devices: none -> 332 us  [on_device(): lax.all_gather(jnp.dot(query_features, precond, preferred_element_type=jn...]
    psum x1 -> x0, blocking collectives: 97.5 us -> none  [on_device(): lax.psum(jnp.dot(query_features, precond, preferred_element_type=jnp.floa...]
    reduce_sum x0 -> x1, other arithmetic: none -> 22.4 us  [on_device(): jnp.sum(lax.all_gather(jnp.dot(query_features, precond, preferred_element...]
  transfers between devices with their start and end apart: 2 -> 3, of which waited for: 2 -> 3; matrix products, arithmetic and copies ran while one was open for 3% -> 2% of each run, Pallas kernels for 0% -> 0%
where the time goes in v2:
time: 638 us
  waiting for transfers between devices  554 us (87%)
  matrix products  26.2 us (4%)
  other arithmetic  22.4 us (4%)
  local copies, waits for them, and re-layouts  17.3 us (3%)
  between operations  13.4 us (2%)
    all_gather x1, waiting for transfers between devices, on_device(): lax.all_gather(jnp.dot(query_features, precond, preferred_element_type=jn...  332 us
    all_to_all x1, waiting for transfers between devices, on_device(): lax.all_to_all(train_features, 'pb', split_axis=0, concat_axis=1, tiled=T...  148 us
    all_gather x1, waiting for transfers between devices, on_device(): lax.all_gather(gathered, 'ex', axis=0, tiled=True)  72.8 us
    dot_general x1, matrix products, tile_product(): lax.dot_general(portion, train_tile, (((1,), (1,)), ((), ())), preferred_...  22.6 us
    reduce_sum x1, other arithmetic, on_device(): jnp.sum(lax.all_gather(jnp.dot(query_features, precond, preferred_element...  22.4 us
  transfers between devices with their start and end apart: 3, of which 3 were waited for; matrix products, arithmetic and copies ran while one was open for 2% of the time, Pallas kernels for 0%

profile of v2, /device:TPU:1, one launch (start us, length us, event | category | flops | bytes accessed | tf_op | source)
XLA Modules:
  0.0 637.7 jit_solution(16114607129717284529)
XLA Ops:
  6.5 0.0 copy-start
  6.5 0.0 all-gather.6.cloned.1.call-start
  6.5 1.6 copy-done
  8.1 3.6 fusion
  11.8 0.0 all-gather.6.cloned.1.call-update
  11.8 0.0 all-gather.4.cloned.1.call-start
  11.8 332.4 %all-gather.6.cloned.1.call-done = f32[4096,4096]{1,0:T(8,128)} async-done(((f32[256,4096]{1,0:T(8,128)}), f32[4096,4096]{1,0:T(8,128)}) %all-gather.6.cloned.1.call-update) | async-done | bytes 67108880 | tf_op jit(solution)/shard_map/all_gather | solution.py:19
  344.2 22.4 %reduce_sum.9 = bf16[256,4096]{1,0:T(8,128)(2,1)} reduce(f32[16,256,4096]{2,1,0:T(8,128)} %bitcast, f32[]{:T(128)} %constant.0.clone.1), dimensions={0}, to_apply=%region_0.0 | reduce | flops 15728640 | bytes 69206016 | tf_op jit(solution)/shard_map/reduce_sum | solution.py:18
  366.6 0.0 all-gather.4.cloned.1.call-update
  366.7 0.0 copy-start.3
  366.7 0.0 copy-start.4
  366.7 4.8 all-to-all-start
  371.4 0.0 copy-done.3
  371.5 0.1 copy.9
  371.5 0.0 copy-done.4
  371.5 148.3 %all-to-all-done = bf16[16,1024,256]{2,1,0:T(8,128)(2,1)} async-done(((bf16[16,1024,256]{2,1,0:T(8,128)(2,1)}), bf16[16,1024,256]{2,1,0:T(8,128)(2,1)}, u32[]{:S(2)}, u32[]{:S(2)}) %all-to-all-start) | async-done | bytes 8388640 | tf_op jit(solution)/shard_map/all_to_all | solution.py:16
  519.8 12.2 %copy.8 = bf16[1024,16,256]{0,2,1:T(8,128)(2,1)} copy(bf16[1024,16,256]{2,0,1:T(8,128)(2,1)} %bitcast.2) | data formatting | bytes 16777216 | tf_op jit(solution)/shard_map/all_to_all | solution.py:16
  532.1 72.8 %all-gather.4.cloned.1.call-done = bf16[2048,4096]{1,0:T(8,128)(2,1)} async-done(((bf16[256,4096]{1,0:T(8,128)(2,1)}), bf16[2048,4096]{1,0:T(8,128)(2,1)}) %all-gather.4.cloned.1.call-update) | async-done | bytes 16777232 | tf_op jit(solution)/shard_map/all_gather | solution.py:24
  604.9 0.0 copy-start.2
  604.9 0.6 mul.29
  605.5 2.8 copy-done.2
  608.3 0.0 copy-start.1
  608.3 22.6 %bitcast_multiply_fusion = f32[2048,1024]{1,0:T(8,128)} fusion(f32[256,8,8,128]{3,2,1,0:T(8,128)S(1)} %bitcast.12, bf16[2048,4096]{1,0:T(8,128)(2,1)} %all-gather.4.cloned.1.call-done, bf16[1024,4096]{0,1:T(8,128)(2,1)S(1)} %bitcast.14, f32[1024]{0:T(1024)S(1)} %broadcast_multiply_fusion), kind=kOutput, calls=%fused_computation | convolution fusion | flops 17184063488 | bytes 41947136 | tf_op jit(solution)/shard_map/dot_general | solution.py:10
  630.9 0.0 copy-done.1
  (2 shorter events, 0.0 us)
Async XLA Ops:
  6.5 1.6 copy-start
  6.5 337.7 %all-gather.6.cloned.1.call-start = ((), (), s32[]{:S(2)}) async-start(), calls=%async_computation.2 | async-start | bytes 71303168 | tf_op jit(solution)/shard_map/all_gather | solution.py:19
  11.8 593.1 %all-gather.4.cloned.1.call-start = ((), (), s32[]{:S(2)}) async-start(), calls=%async_computation.1 | async-start | bytes 18874368 | tf_op jit(solution)/shard_map/all_gather | solution.py:24
  366.7 4.8 copy-start.3
  366.7 4.9 copy-start.4
  366.7 153.1 %all-to-all-start = ((bf16[16,1024,256]{2,1,0:T(8,128)(2,1)}), bf16[16,1024,256]{2,1,0:T(8,128)(2,1)}, u32[]{:S(2)}, u32[]{:S(2)}) async-start(bf16[16,1024,256]{2,1,0:T(8,128)(2,1)} %bitcast.13), calls=%async_computation | async-start | bytes 16777216 | tf_op jit(solution)/shard_map/all_to_all | solution.py:16
  604.9 3.4 copy-start.2
  608.3 22.6 %copy-start.1 = (bf16[256,4096]{1,0:T(8,128)(2,1)S(1)}, bf16[256,4096]{1,0:T(8,128)(2,1)}, u32[]{:S(2)}) copy-start(bf16[256,4096]{1,0:T(8,128)(2,1)} %param.7) | copy-start | bytes 6291460
Sparse Core Ops, SparseCore 0:
  11.9 332.2 all-gather.5
  366.8 238.0 all-gather.3
